TPU v7x, 256 devices: a whole 4x4x8 slice. The times are simulated.
256 devices in a mesh: ctx: 64 (over x, y, z_lo), tp: 4 (over z_hi, core).
Axes of the slice: x: 4, y: 4, z: 8 (z_hi: 2, z_lo: 4; z = z_hi * 4 + z_lo), core: 2. Of those that a mesh axis runs over, the one named last changes fastest.
Arguments:
- span_rows: bfloat16 [2, 2048, 3584], P(None, 'ctx'), may hold values from -6 to 6
- step_rows: bfloat16 [4, 256, 3584], P(None, 'ctx'), may hold values from -6 to 6
- lengths: int32 [2], replicated, may hold values from 4097 to 6144
- sample_prompt: int32 [256], P('ctx'), may hold values from 0 to 1
- norm_gain: float32 [3584], replicated, may hold values from 0.5 to 1.5
- query_weight: bfloat16 [3584, 3584], P('ctx', 'tp'), may hold values from -0.1875 to 0.1875
- key_weight: bfloat16 [3584, 512], P(None, 'tp'), may hold values from -0.1875 to 0.1875
- value_weight: bfloat16 [3584, 512], P(None, 'tp'), may hold values from -0.09375 to 0.09375
- query_bias: float32 [3584], P('tp'), may hold values from -16 to 16
- key_bias: float32 [512], P('tp'), may hold values from -16 to 16
- value_bias: float32 [512], P('tp'), may hold values from -3 to 3
- out_weight: bfloat16 [3584, 3584], P('tp', 'ctx'), may hold values from -0.25 to 0.25
- cache_keys: bfloat16 [2, 4096, 512], P(None, 'ctx', 'tp'), may hold values from -12 to 12
- cache_values: bfloat16 [2, 4096, 512], P(None, 'ctx', 'tp'), may hold values from -6 to 6
Outputs:
- span_out: bfloat16 [2, 2048, 3584], P(None, 'ctx', 'tp')
- dec_out: bfloat16 [4, 256, 3584], P(None, 'ctx', 'tp')
All inputs are finite; a program needn't handle non-finite values.
Results may differ from a plain program's by a relative error of at most 0.012.
The roundings to bfloat16 on the way count: a program that leaves them out, or rounds other values in their place, can miss the bound.
Values may be sent and summed in bfloat16 or wider, within the bound.
A program may use at most 128 MiB of HBM per device.

v0:
```python
import math
import jax
import jax.numpy as jnp
from jax import lax
from jax.sharding import PartitionSpec as P

HEADS = 28
KV_HEADS = 4
HEAD = 128
ROPE_BASE = 1000000.0
NORM_EPS = 1e-06
MASKED = -1e30


def turned_gather(arrays, axis, dims):
    turned = [jnp.moveaxis(a, dim, 0) for a, dim in zip(arrays, dims)]
    widths = [t[0].size for t in turned]
    both = jnp.concatenate([t.reshape(-1, w) for t, w in zip(turned, widths)], axis=1)
    filled = lax.all_gather(both, axis, axis=0, tiled=True)
    parts = jnp.split(filled, [sum(widths[:k]) for k in range(1, len(widths))], axis=1)
    return tuple(
        (
            jnp.moveaxis(b.reshape(-1, *t.shape[1:]), 0, dim)
            for b, t, dim in zip(parts, turned, dims)
        )
    )


def sent_together(arrays, axis, dim, along):
    widths = [a.shape[along] for a in arrays]
    both = jnp.concatenate(arrays, axis=along)
    filled = lax.all_gather(both, axis, axis=dim, tiled=True)
    return tuple(jnp.split(filled, [sum(widths[:k]) for k in range(1, len(widths))], axis=along))


def in_blocks(x, dim, length):
    before, after = (x.shape[:dim], x.shape[dim + 1 :])
    return jnp.moveaxis(x.reshape(*before, length, -1, *after), dim, 0)


def sum_at_owner(x, axis, dim):
    parts = in_blocks(x, dim, lax.axis_size(axis))
    arrived = lax.all_to_all(parts, axis, split_axis=0, concat_axis=0, tiled=True)
    return arrived.astype(jnp.float32).sum(axis=0)


def norm_rows(inputs, norm_gain):
    widened = inputs.astype(jnp.float32)
    inverse = lax.rsqrt(jnp.mean(widened * widened, axis=-1, keepdims=True) + NORM_EPS)
    return (widened * inverse * norm_gain).astype(jnp.bfloat16)


def rotate(vectors, positions):
    width = vectors.shape[-1]
    half = width // 2
    exponent = jnp.arange(half, dtype=jnp.float32) * (2.0 / width)
    frequency = jnp.exp(exponent * -math.log(ROPE_BASE))
    angles = positions.astype(jnp.float32)[..., None, None] * frequency
    cosine = jnp.cos(angles)
    sine = jnp.sin(angles)
    first = vectors[..., :half]
    second = vectors[..., half:]
    return jnp.concatenate(
        [first * cosine - second * sine, second * cosine + first * sine], axis=-1
    )


def project(normed, weight, bias):
    return jnp.dot(normed, weight, preferred_element_type=jnp.float32) + bias


def key_positions(count, prefix_dev, span_dev, prefix_all):
    row_index = jnp.arange(count, dtype=jnp.int32)
    device = row_index // (prefix_dev + span_dev)
    offset = row_index % (prefix_dev + span_dev)
    return jnp.where(
        offset < prefix_dev,
        device * prefix_dev + offset,
        prefix_all + device * span_dev + offset - prefix_dev,
    )


def local(
    span_rows,
    step_rows,
    lengths,
    sample_prompt,
    norm_gain,
    query_weight,
    key_weight,
    value_weight,
    query_bias,
    key_bias,
    value_bias,
    out_weight,
    cache_keys,
    cache_values,
):
    cycle_size = lax.axis_size("ctx")
    cycle_place = lax.axis_index("ctx")
    prompt_count = span_rows.shape[0]
    span_dev = span_rows.shape[1]
    prefix_dev = cache_keys.shape[1]
    kv_local = key_weight.shape[1] // HEAD
    kv_group = HEADS // KV_HEADS
    heads_local = kv_local * kv_group
    prefix_all = prefix_dev * cycle_size
    factor = HEAD ** (-0.5)
    full_query, full_out = turned_gather((query_weight, out_weight), "ctx", (0, 1))
    normed = norm_rows(span_rows, norm_gain)
    span_places = prefix_all + cycle_place * span_dev + jnp.arange(span_dev, dtype=jnp.int32)
    grid_places = jnp.broadcast_to(span_places, (prompt_count, span_dev))
    queries = rotate(
        project(normed, full_query, query_bias).reshape(prompt_count, span_dev, heads_local, HEAD),
        grid_places,
    ).astype(jnp.bfloat16)
    new_keys = rotate(
        project(normed, key_weight, key_bias).reshape(prompt_count, span_dev, kv_local, HEAD),
        grid_places,
    ).astype(jnp.bfloat16)
    new_values = project(normed, value_weight, value_bias).astype(jnp.bfloat16)
    key_block = jnp.concatenate(
        [cache_keys, new_keys.reshape(prompt_count, span_dev, kv_local * HEAD)], axis=1
    )
    value_block = jnp.concatenate([cache_values, new_values], axis=1)
    query_rows = (
        queries.reshape(prompt_count, span_dev, kv_local, kv_group, HEAD)
        .transpose(0, 2, 1, 3, 4)
        .reshape(prompt_count, kv_local, span_dev * kv_group, HEAD)
    )
    query_places = jnp.repeat(span_places, kv_group)
    row_count = span_dev * kv_group
    key_all, value_all = sent_together((key_block, value_block), "ctx", 1, 0)
    highest = jnp.full((prompt_count, kv_local, row_count), MASKED, jnp.float32)
    count = key_all.shape[1]
    places = key_positions(count, prefix_dev, span_dev, prefix_all)
    key_grid = key_all.reshape(prompt_count, count, kv_local, HEAD)
    value_grid = value_all.reshape(prompt_count, count, kv_local, HEAD)
    scores = (
        jnp.einsum("pgqd,pkgd->pgqk", query_rows, key_grid, preferred_element_type=jnp.float32)
        * factor
    )
    visible = (places[None, None, None, :] < lengths[:, None, None, None]) & (
        places[None, None, None, :] <= query_places[None, None, :, None]
    )
    scores = jnp.where(visible, scores, MASKED)
    raised = jnp.maximum(highest, jnp.max(scores, axis=-1))
    weights = jnp.where(visible, jnp.exp(scores - raised[..., None]), 0.0)
    totals = jnp.sum(weights, axis=-1)
    blended = jnp.einsum(
        "pgqk,pkgd->pgqd",
        weights.astype(jnp.bfloat16),
        value_grid,
        preferred_element_type=jnp.float32,
    )
    highest, totals, blended = (raised, totals, blended)
    span_attention = (blended / totals[..., None]).astype(jnp.bfloat16)
    span_attention = (
        span_attention.reshape(prompt_count, kv_local, span_dev, kv_group, HEAD)
        .transpose(0, 2, 1, 3, 4)
        .reshape(prompt_count, span_dev, heads_local * HEAD)
    )
    span_terms = jnp.dot(span_attention, full_out, preferred_element_type=jnp.float32)
    span_out = sum_at_owner(span_terms.astype(jnp.bfloat16), "tp", 2).astype(jnp.bfloat16)
    gathered_rows = key_all.shape[1]
    key_grid = key_all.reshape(prompt_count, gathered_rows, kv_local, HEAD)
    value_grid = value_all.reshape(prompt_count, gathered_rows, kv_local, HEAD)
    all_places = key_positions(gathered_rows, prefix_dev, span_dev, prefix_all)
    picked = sample_prompt[:, None] == jnp.arange(prompt_count, dtype=jnp.int32)[None, :]
    length_of = jnp.sum(jnp.where(picked, lengths[None, :], 0), axis=1)
    prefix_visible = picked[:, :, None] & (all_places[None, None, :] < length_of[:, None, None])
    wide_visible = prefix_visible[:, None, None, :, :]
    sample_count = step_rows.shape[1]
    step_count = step_rows.shape[0]
    step_ids = jnp.arange(step_count, dtype=jnp.int32)
    made_keys = jnp.zeros((sample_count, step_count, kv_local, HEAD), jnp.bfloat16)
    made_values = jnp.zeros((sample_count, step_count, kv_local, HEAD), jnp.bfloat16)
    outputs = []
    for step_index in range(step_count):
        normed_step = norm_rows(step_rows[step_index], norm_gain)
        places_now = length_of + step_index
        step_queries = rotate(
            project(normed_step, full_query, query_bias).reshape(sample_count, heads_local, HEAD),
            places_now,
        ).astype(jnp.bfloat16)
        step_queries = step_queries.reshape(sample_count, kv_local, kv_group, HEAD)
        fresh_keys = rotate(
            project(normed_step, key_weight, key_bias).reshape(sample_count, kv_local, HEAD),
            places_now,
        ).astype(jnp.bfloat16)
        fresh_values = (
            project(normed_step, value_weight, value_bias)
            .astype(jnp.bfloat16)
            .reshape(sample_count, kv_local, HEAD)
        )
        made_keys = made_keys.at[:, step_index].set(fresh_keys)
        made_values = made_values.at[:, step_index].set(fresh_values)
        own_visible = step_ids <= step_index
        far_scores = (
            jnp.einsum(
                "sgqd,pkgd->sgqpk", step_queries, key_grid, preferred_element_type=jnp.float32
            )
            * factor
        )
        far_scores = jnp.where(wide_visible, far_scores, MASKED)
        near_scores = (
            jnp.einsum(
                "sgqd,stgd->sgqt", step_queries, made_keys, preferred_element_type=jnp.float32
            )
            * factor
        )
        near_scores = jnp.where(own_visible, near_scores, MASKED)
        highest_now = jnp.maximum(jnp.max(far_scores, axis=(3, 4)), jnp.max(near_scores, axis=-1))
        far_weights = jnp.where(
            wide_visible, jnp.exp(far_scores - highest_now[..., None, None]), 0.0
        )
        near_weights = jnp.where(own_visible, jnp.exp(near_scores - highest_now[..., None]), 0.0)
        totals_now = jnp.sum(far_weights, axis=(3, 4)) + jnp.sum(near_weights, axis=-1)
        blended_now = jnp.einsum(
            "sgqpk,pkgd->sgqd",
            far_weights.astype(jnp.bfloat16),
            value_grid,
            preferred_element_type=jnp.float32,
        )
        blended_now = blended_now + jnp.einsum(
            "sgqt,stgd->sgqd",
            near_weights.astype(jnp.bfloat16),
            made_values,
            preferred_element_type=jnp.float32,
        )
        step_attention = (
            (blended_now / totals_now[..., None])
            .astype(jnp.bfloat16)
            .reshape(sample_count, heads_local * HEAD)
        )
        outputs.append(step_attention)
    stacked = jnp.stack(outputs)
    decode_terms = jnp.dot(stacked, full_out, preferred_element_type=jnp.float32)
    dec_out = sum_at_owner(decode_terms.astype(jnp.bfloat16), "tp", 2).astype(jnp.bfloat16)
    return (span_out, dec_out)


def solution(mesh):
    return jax.shard_map(
        local,
        mesh=mesh,
        in_specs=(
            P(None, "ctx", None),
            P(None, "ctx", None),
            P(),
            P("ctx"),
            P(),
            P("ctx", "tp"),
            P(None, "tp"),
            P(None, "tp"),
            P("tp"),
            P("tp"),
            P("tp"),
            P("tp", "ctx"),
            P(None, "ctx", "tp"),
            P(None, "ctx", "tp"),
        ),
        out_specs=(P(None, "ctx", "tp"), P(None, "ctx", "tp")),
        check_vma=False,
    )
```

profile of v0, /device:TPU:1, one launch (start us, length us, event | category | flops | bytes accessed | tf_op | source)
XLA Modules:
  0.0 852.5 jit_solution(219215414746392253)
XLA Ops:
  7.3 1.8 pad_maximum_fusion
  9.2 1.2 fusion.129
  10.4 1.7 fusion.62
  12.2 1.4 fusion.63
  13.6 0.7 maximum_maximum_fusion
  14.9 0.3 fusion.118
  15.3 0.3 fusion.107
  15.8 0.3 fusion.104
  16.1 0.3 fusion.105
  16.4 0.3 fusion.106
  17.4 2.0 broadcast_compare_fusion
  19.4 345.0 %all-gather.3.cloned.1.call-done = bf16[3584,1792]{1,0:T(8,128)(2,1)} async-done(((bf16[56,1792]{1,0:T(8,128)(2,1)}), bf16[3584,1792]{1,0:T(8,128)(2,1)}) %all-gather.3.cloned.1.call-update) | async-done | bytes 12845072 | tf_op jit(solution)/shard_map/all_gather | solution.py:19
  364.5 3.8 fusion.91
  368.3 3.8 fusion.88
  372.1 3.8 fusion.94
  376.0 3.8 fusion.97
  380.1 350.8 %all-gather.5.cloned.1.call-done = bf16[4,6144,128]{2,1,0:T(8,128)(2,1)} async-done(((bf16[4,96,128]{2,1,0:T(8,128)(2,1)}), bf16[4,6144,128]{2,1,0:T(8,128)(2,1)}) %all-gather.5.cloned.1.call-update) | async-done | bytes 6291472 | tf_op jit(solution)/shard_map/all_gather | solution.py:32
  730.9 3.3 fusion.310
  734.6 1.3 fusion.312
  736.3 1.3 fusion.314
  737.7 0.8 fusion.309
  738.5 1.3 fusion.308
  740.0 1.8 fusion.51
  741.8 0.6 fusion.64
  742.4 0.2 fusion.87
  742.6 0.3 fusion.117
  743.0 0.8 fusion.67
  743.9 0.2 fusion.86
  744.1 0.3 fusion.115
  744.4 0.6 fusion.70
  745.1 0.2 fusion.85
  745.3 0.3 fusion.113
  745.7 4.1 fusion.59
  750.3 4.8 fusion.307
  755.2 3.0 fusion
  758.2 5.2 fusion.124
  763.7 3.0 fusion.73
  766.7 0.2 fusion.84
  767.0 4.7 fusion.19
  771.6 0.7 copy.96
  772.3 47.0 %all-to-all-start.1 = ((bf16[4,4,4,896]{3,2,1,0:T(4,128)(2,1)}), bf16[4,4,4,896]{3,2,1,0:T(4,128)(2,1)S(1)}, u32[]{:S(2)}, u32[]{:S(2)}) async-start(bf16[4,4,4,896]{3,2,1,0:T(4,128)(2,1)} %bitcast.277), calls=%async_computation.1 | async-start | bytes 229376 | tf_op jit(solution)/shard_map/all_to_all | solution.py:43
  819.3 4.9 fusion.18
  824.2 0.8 copy.95
  825.1 1.6 all-to-all-done.1
  826.7 5.6 all-to-all-start
  832.3 0.7 reduce_sum.175
  832.9 12.0 %all-to-all-done = bf16[4,2,32,896]{3,2,1,0:T(8,128)(2,1)S(1)} async-done(((bf16[4,2,32,896]{3,2,1,0:T(8,128)(2,1)}), bf16[4,2,32,896]{3,2,1,0:T(8,128)(2,1)S(1)}, u32[]{:S(2)}, u32[]{:S(2)}) %all-to-all-start) | async-done | bytes 458784 | tf_op jit(solution)/shard_map/all_to_all | solution.py:43
  844.9 0.7 reduce_sum.161
  (104 shorter events, 4.3 us)
Async XLA Ops:
  7.2 5.1 copy-start
  7.2 7.6 copy-start.3
  7.2 8.1 copy-start.1
  7.2 8.1 copy-start.10
  7.2 7.6 copy-start.11
  7.2 6.4 copy-start.8
  7.2 6.4 copy-start.9
  7.3 7.4 copy-start.4
  7.3 7.9 copy-start.13
  7.3 7.9 copy-start.17
  7.3 357.2 %all-gather.3.cloned.1.call-start = ((), (), s32[]{:S(2)}) async-start(), calls=%async_computation.2 | async-start | bytes 13045760 | tf_op jit(solution)/shard_map/all_gather | solution.py:19
  9.1 721.8 %all-gather.5.cloned.1.call-start = ((), (), s32[]{:S(2)}) async-start(), calls=%async_computation.3 | async-start | bytes 6389760 | tf_op jit(solution)/shard_map/all_gather | solution.py:32
  14.6 723.1 %copy-start.14 = (pred[4]{0:T(512)(128)(4,1)}, pred[4]{0:T(512)(128)(4,1)S(1)}, u32[]{:S(2)}) copy-start(pred[4]{0:T(512)(128)(4,1)S(1)} %iota_compare_fusion.2) | copy-start | bytes 16
  14.8 349.6 %copy-start.7 = (f32[896]{0:T(1024)S(1)}, f32[896]{0:T(1024)}, u32[]{:S(2)}) copy-start(f32[896]{0:T(1024)} %param.38) | copy-start | bytes 10756
  730.9 3.7 copy-start.16
  739.8 2.0 copy-start.5
  744.4 1.3 copy-start.6
  750.3 4.9 copy-start.2
  758.2 5.4 copy-start.12
  758.2 5.4 copy-start.15
  772.3 54.4 %all-to-all-start.1 = ((bf16[4,4,4,896]{3,2,1,0:T(4,128)(2,1)}), bf16[4,4,4,896]{3,2,1,0:T(4,128)(2,1)S(1)}, u32[]{:S(2)}, u32[]{:S(2)}) async-start(bf16[4,4,4,896]{3,2,1,0:T(4,128)(2,1)} %bitcast.277), calls=%async_computation.1 | async-start | bytes 229376 | tf_op jit(solution)/shard_map/all_to_all | solution.py:43
  826.7 18.3 %all-to-all-start = ((bf16[4,2,32,896]{3,2,1,0:T(8,128)(2,1)}), bf16[4,2,32,896]{3,2,1,0:T(8,128)(2,1)S(1)}, u32[]{:S(2)}, u32[]{:S(2)}) async-start(bf16[4,2,32,896]{3,2,1,0:T(8,128)(2,1)} %bitcast.275), calls=%async_computation | async-start | bytes 917504 | tf_op jit(solution)/shard_map/all_to_all | solution.py:43
Sparse Core Ops, SparseCore 0:
  9.9 354.5 all-gather.2
  366.8 363.9 all-gather.4
where the time goes:
time: 853 us; the launch traced here: 852 us
  waiting for transfers between devices  709 us (83%)
  matrix products  58.9 us (7%)
  starting transfers between devices  52.7 us (6%)
  between operations  14.6 us (2%)
  other arithmetic  14.3 us (2%)
    all_gather x1, waiting for transfers between devices, sent_together(): filled = lax.all_gather(both, axis, axis=dim, tiled=True)  351 us
    all_gather x1, waiting for transfers between devices, turned_gather(): filled = lax.all_gather(both, axis, axis=0, tiled=True)  345 us
    all_to_all x2, starting transfers between devices, sum_at_owner(): lax.all_to_all(parts, axis, split_axis=0, concat_axis=0, tiled=True)  52.6 us
    dot_general x15, matrix products, project(): return jnp.dot(normed, weight, preferred_element_type=jnp.float32) + bias  24.7 us
  transfers between devices with their start and end apart: 4, of which 4 were waited for; matrix products, arithmetic and copies ran while one was open for 4% of the time, Pallas kernels for 0%

commit v1 on v0

--- a/solution.py
+++ b/solution.py
@@ -16,7 +16,9 @@
     turned = [jnp.moveaxis(a, dim, 0) for a, dim in zip(arrays, dims)]
     widths = [t[0].size for t in turned]
     both = jnp.concatenate([t.reshape(-1, w) for t, w in zip(turned, widths)], axis=1)
-    filled = lax.all_gather(both, axis, axis=0, tiled=True)
+    filled = jnp.concatenate(
+        lax.all_to_all(jnp.stack([both] * lax.axis_size(axis)), axis, 0, 0), axis=0
+    )
     parts = jnp.split(filled, [sum(widths[:k]) for k in range(1, len(widths))], axis=1)
     return tuple(
         (

time: 853 us -> 570 us (0.67)
  waiting for transfers between devices: 709 us -> 420 us
    all_to_all x0 -> x1, waiting for transfers between devices: none -> 385 us  [turned_gather(): lax.all_to_all(jnp.stack([both] * lax.axis_size(axis)), axis, 0, 0)]
    all_gather x1 -> x0, waiting for transfers between devices: 345 us -> none  [turned_gather(): filled = lax.all_gather(both, axis, axis=0, tiled=True)]
    all_gather x1, waiting for transfers between devices: 351 us -> 24.5 us  [sent_together(): filled = lax.all_gather(both, axis, axis=dim, tiled=True)]
    all_to_all x0 -> x1, starting transfers between devices: none -> 12.9 us  [turned_gather(): lax.all_to_all(jnp.stack([both] * lax.axis_size(axis)), axis, 0, 0)]
    all_to_all x2, starting transfers between devices: 52.6 us -> 43.7 us  [sum_at_owner(): lax.all_to_all(parts, axis, split_axis=0, concat_axis=0, tiled=True)]
  transfers between devices with their start and end apart: 4 -> 4, of which waited for: 4 -> 3; matrix products, arithmetic and copies ran while one was open for 4% -> 8% of each run, Pallas kernels for 0% -> 0%
where the time goes in v1:
time: 570 us; the launch traced here: 569 us
  waiting for transfers between devices  420 us (74%)
  starting transfers between devices  56.6 us (10%)
  matrix products  55.4 us (10%)
  between operations  14.7 us (3%)
  other arithmetic  13.8 us (2%)
  local copies, waits for them, and re-layouts  8.98 us (2%)
    all_to_all x1, waiting for transfers between devices, turned_gather(): lax.all_to_all(jnp.stack([both] * lax.axis_size(axis)), axis, 0, 0)  385 us
    all_to_all x2, starting transfers between devices, sum_at_owner(): lax.all_to_all(parts, axis, split_axis=0, concat_axis=0, tiled=True)  43.7 us
    all_gather x1, waiting for transfers between devices, sent_together(): filled = lax.all_gather(both, axis, axis=dim, tiled=True)  24.5 us
    dot_general x15, matrix products, project(): return jnp.dot(normed, weight, preferred_element_type=jnp.float32) + bias  22.4 us
    all_to_all x1, starting transfers between devices, turned_gather(): lax.all_to_all(jnp.stack([both] * lax.axis_size(axis)), axis, 0, 0)  12.9 us
  transfers between devices with their start and end apart: 4, of which 3 were waited for; matrix products, arithmetic and copies ran while one was open for 8% of the time, Pallas kernels for 0%

profile of v1, /device:TPU:1, one launch (start us, length us, event | category | flops | bytes accessed | tf_op | source)
XLA Modules:
  0.0 569.3 jit_solution(8174812874599158945)
XLA Ops:
  7.2 1.0 pad_maximum_fusion
  8.2 5.4 stack.4
  13.7 12.9 %all-to-all-start = ((bf16[64,56,1792]{2,1,0:T(8,128)(2,1)}), bf16[64,56,1792]{2,1,0:T(8,128)(2,1)}, u32[]{:S(2)}, u32[]{:S(2)}) async-start(bf16[64,56,1792]{2,1,0:T(8,128)(2,1)} %stack.4), calls=%async_computation | async-start | bytes 25690112 | tf_op jit(solution)/shard_map/all_to_all | solution.py:20
  27.0 0.3 fusion.62
  27.5 0.3 fusion.63
  27.8 0.7 maximum_maximum_fusion
  29.1 0.3 fusion.118
  29.3 0.6 pad_bitcast_fusion
  30.0 0.3 fusion.107
  30.6 0.3 fusion.104
  30.9 0.3 fusion.105
  31.2 0.3 fusion.106
  31.8 0.8 multiply_cosine_fusion.1
  32.6 0.7 broadcast_compare_fusion.2
  33.5 2.0 broadcast_compare_fusion
  35.4 384.9 %all-to-all-done = bf16[64,56,1792]{2,1,0:T(8,128)(2,1)} async-done(((bf16[64,56,1792]{2,1,0:T(8,128)(2,1)}), bf16[64,56,1792]{2,1,0:T(8,128)(2,1)}, u32[]{:S(2)}, u32[]{:S(2)}) %all-to-all-start) | async-done | bytes 12845088 | tf_op jit(solution)/shard_map/all_to_all | solution.py:20
  420.3 3.8 fusion.88
  424.2 3.8 fusion.91
  428.0 3.8 fusion.94
  431.9 3.8 fusion.97
  437.0 24.5 %all-gather.2.cloned.1.call-done = bf16[4,6144,128]{2,1,0:T(8,128)(2,1)} async-done(((bf16[4,96,128]{2,1,0:T(8,128)(2,1)}), bf16[4,6144,128]{2,1,0:T(8,128)(2,1)}) %all-gather.2.cloned.1.call-update) | async-done | bytes 6291472 | tf_op jit(solution)/shard_map/all_gather | solution.py:34
  461.6 3.3 fusion.308
  464.9 0.4 copy-done.29
  465.3 1.3 fusion.314
  466.6 1.3 fusion.312
  467.9 1.3 fusion.310
  469.5 1.8 fusion.51
  471.3 0.6 fusion.64
  472.2 0.4 fusion.117
  472.6 0.6 fusion.67
  473.2 0.2 fusion.86
  473.5 0.3 fusion.115
  473.8 0.6 fusion.70
  474.7 0.3 fusion.113
  475.1 4.1 fusion.59
  479.3 2.5 fusion.73
  482.1 4.7 fusion.19
  486.8 0.7 copy.96
  487.5 36.5 %all-to-all-start.2 = ((bf16[4,4,4,896]{3,2,1,0:T(4,128)(2,1)}), bf16[4,4,4,896]{3,2,1,0:T(4,128)(2,1)S(1)}, u32[]{:S(2)}, u32[]{:S(2)}) async-start(bf16[4,4,4,896]{3,2,1,0:T(4,128)(2,1)} %bitcast.278), calls=%async_computation.2 | async-start | bytes 229376 | tf_op jit(solution)/shard_map/all_to_all | solution.py:45
  524.6 4.8 fusion.307
  529.4 3.0 fusion
  532.4 5.2 fusion.124
  537.8 4.9 fusion.18
  542.7 0.8 copy.95
  543.5 7.2 %all-to-all-start.1 = ((bf16[4,2,32,896]{3,2,1,0:T(8,128)(2,1)}), bf16[4,2,32,896]{3,2,1,0:T(8,128)(2,1)S(1)}, u32[]{:S(2)}, u32[]{:S(2)}) async-start(bf16[4,2,32,896]{3,2,1,0:T(8,128)(2,1)} %bitcast.276), calls=%async_computation.1 | async-start | bytes 917504 | tf_op jit(solution)/shard_map/all_to_all | solution.py:45
  550.7 0.7 reduce_sum.175
  551.4 10.4 %all-to-all-done.1 = bf16[4,2,32,896]{3,2,1,0:T(8,128)(2,1)S(1)} async-done(((bf16[4,2,32,896]{3,2,1,0:T(8,128)(2,1)}), bf16[4,2,32,896]{3,2,1,0:T(8,128)(2,1)S(1)}, u32[]{:S(2)}, u32[]{:S(2)}) %all-to-all-start.1) | async-done | bytes 458784 | tf_op jit(solution)/shard_map/all_to_all | solution.py:45
  561.8 0.7 reduce_sum.161
  (130 shorter events, 5.0 us)
Async XLA Ops:
  7.2 20.3 %copy-start = (bf16[3584,128]{1,0:T(8,128)(2,1)S(1)}, bf16[3584,128]{1,0:T(8,128)(2,1)}, u32[]{:S(2)}) copy-start(bf16[3584,128]{1,0:T(8,128)(2,1)} %param.37) | copy-start | bytes 2752516
  13.6 13.1 %copy-start.5 = (bf16[2,32,3584]{2,1,0:T(8,128)(2,1)S(1)}, bf16[2,32,3584]{2,1,0:T(8,128)(2,1)}, u32[]{:S(2)}) copy-start(bf16[2,32,3584]{2,1,0:T(8,128)(2,1)} %param.30) | copy-start | bytes 1376260
  13.7 13.3 %copy-start.1 = (bf16[3584,128]{1,0:T(8,128)(2,1)S(1)}, bf16[3584,128]{1,0:T(8,128)(2,1)}, u32[]{:S(2)}) copy-start(bf16[3584,128]{1,0:T(8,128)(2,1)} %param.36) | copy-start | bytes 2752516
  13.7 13.3 %copy-start.3 = (f32[3584]{0:T(1024)S(1)}, f32[3584]{0:T(1024)}, u32[]{:S(2)}) copy-start(f32[3584]{0:T(1024)} %param.34) | copy-start | bytes 43012
  13.7 13.3 %copy-start.13 = (f32[128]{0:T(128)S(1)}, f32[128]{0:T(128)}, u32[]{:S(2)}) copy-start(f32[128]{0:T(128)} %param.39) | copy-start | bytes 1540
  13.7 13.8 %copy-start.14 = (f32[128]{0:T(128)S(1)}, f32[128]{0:T(128)}, u32[]{:S(2)}) copy-start(f32[128]{0:T(128)} %param.40) | copy-start | bytes 1540
  13.7 406.6 %all-to-all-start = ((bf16[64,56,1792]{2,1,0:T(8,128)(2,1)}), bf16[64,56,1792]{2,1,0:T(8,128)(2,1)}, u32[]{:S(2)}, u32[]{:S(2)}) async-start(bf16[64,56,1792]{2,1,0:T(8,128)(2,1)} %stack.4), calls=%async_computation | async-start | bytes 25690112 | tf_op jit(solution)/shard_map/all_to_all | solution.py:20
  26.6 1.2 copy-start.11
  26.6 1.2 copy-start.12
  26.6 2.0 copy-start.4
  26.6 3.3 copy-start.20
  26.6 3.3 copy-start.30
  26.7 434.9 %all-gather.2.cloned.1.call-start = ((), (), s32[]{:S(2)}) async-start(), calls=%async_computation.3 | async-start | bytes 6389760 | tf_op jit(solution)/shard_map/all_gather | solution.py:34
  27.0 3.9 copy-start.18
  28.6 407.2 %copy-start.27 = (pred[4]{0:T(512)(128)(4,1)}, pred[4]{0:T(512)(128)(4,1)S(1)}, u32[]{:S(2)}) copy-start(pred[4]{0:T(512)(128)(4,1)S(1)} %iota_compare_fusion.5) | copy-start | bytes 16
  28.6 407.5 %copy-start.25 = (pred[4]{0:T(512)(128)(4,1)}, pred[4]{0:T(512)(128)(4,1)S(1)}, u32[]{:S(2)}) copy-start(pred[4]{0:T(512)(128)(4,1)S(1)} %iota_compare_fusion.4) | copy-start | bytes 16
  28.6 407.8 %copy-start.23 = (pred[4]{0:T(512)(128)(4,1)}, pred[4]{0:T(512)(128)(4,1)S(1)}, u32[]{:S(2)}) copy-start(pred[4]{0:T(512)(128)(4,1)S(1)} %iota_compare_fusion.3) | copy-start | bytes 16
  28.9 408.0 %copy-start.21 = (pred[4]{0:T(512)(128)(4,1)}, pred[4]{0:T(512)(128)(4,1)S(1)}, u32[]{:S(2)}) copy-start(pred[4]{0:T(512)(128)(4,1)S(1)} %iota_compare_fusion.2) | copy-start | bytes 16
  29.1 391.3 %copy-start.10 = (f32[896]{0:T(1024)S(1)}, f32[896]{0:T(1024)}, u32[]{:S(2)}) copy-start(f32[896]{0:T(1024)} %param.38) | copy-start | bytes 10756
  31.2 393.0 %copy-start.15 = (f32[4]{0:T(128)}, f32[4]{0:T(128)S(1)}, u32[]{:S(2)}) copy-start(f32[4]{0:T(128)S(1)} %add_rsqrt_fusion.3) | copy-start | bytes 52
  461.6 3.7 copy-start.29
  467.9 1.3 copy-start.24
  467.9 1.4 copy-start.26
  467.9 1.5 copy-start.28
  471.3 0.7 copy-start.17
  471.3 0.9 copy-start.16
  473.8 1.3 copy-start.6
  473.8 1.3 copy-start.19
  475.1 4.1 copy-start.22
  482.1 41.9 %copy-start.7 = (f32[2,32,64]{2,1,0:T(8,128)S(1)}, f32[2,32,64]{2,1,0:T(8,128)}, u32[]{:S(2)}) copy-start(f32[2,32,64]{2,1,0:T(8,128)} %get-tuple-element.134) | copy-start | bytes 49156
  482.1 41.9 %copy-start.8 = (f32[2,32,64]{2,1,0:T(8,128)S(1)}, f32[2,32,64]{2,1,0:T(8,128)}, u32[]{:S(2)}) copy-start(f32[2,32,64]{2,1,0:T(8,128)} %get-tuple-element.135) | copy-start | bytes 49156
  482.1 42.4 %copy-start.9 = (pred[2,6144]{1,0:T(4,128)(4,1)S(1)}, pred[2,6144]{1,0:T(4,128)(4,1)}, u32[]{:S(2)}) copy-start(pred[2,6144]{1,0:T(4,128)(4,1)} %broadcast_compare_fusion.2) | copy-start | bytes 36868
  487.5 56.0 %all-to-all-start.2 = ((bf16[4,4,4,896]{3,2,1,0:T(4,128)(2,1)}), bf16[4,4,4,896]{3,2,1,0:T(4,128)(2,1)S(1)}, u32[]{:S(2)}, u32[]{:S(2)}) async-start(bf16[4,4,4,896]{3,2,1,0:T(4,128)(2,1)} %bitcast.278), calls=%async_computation.2 | async-start | bytes 229376 | tf_op jit(solution)/shard_map/all_to_all | solution.py:45
  524.6 4.9 copy-start.2
  543.5 18.2 %all-to-all-start.1 = ((bf16[4,2,32,896]{3,2,1,0:T(8,128)(2,1)}), bf16[4,2,32,896]{3,2,1,0:T(8,128)(2,1)S(1)}, u32[]{:S(2)}, u32[]{:S(2)}) async-start(bf16[4,2,32,896]{3,2,1,0:T(8,128)(2,1)} %bitcast.276), calls=%async_computation.1 | async-start | bytes 917504 | tf_op jit(solution)/shard_map/all_to_all | solution.py:45
Sparse Core Ops, SparseCore 0:
  29.8 431.7 all-gather.1
